TPU v7x, 32 devices: a whole 2x2x4 slice. The times are simulated.
32 devices in a mesh: fsdp: 4 (over x, core), ctx: 4 (over z), tp: 2 (over y).
Axes of the slice: x: 2, y: 2, z: 4, core: 2. Of those that a mesh axis runs over, the one named last changes fastest.
Arguments:
- tokens: bfloat16 [4, 2048, 1536], P('fsdp', 'ctx'), may hold values from -6 to 6
- segments: int32 [4, 2048], P('fsdp', 'ctx'), may hold values from 0 to 7, never falling along the last dimension, each value on 1 to 800 neighbouring positions
- adapter_index: int32 [4], P('fsdp'), may hold values from 0 to 7
- w_qkv: bfloat16 [1536, 3, 1536], P('fsdp', None, 'tp'), may hold values from -0.15625 to 0.15625
- w_forget: bfloat16 [1536, 24], P('fsdp', 'tp'), may hold values from -0.4375 to 0.4375
- forget_bias: bfloat16 [24], P('tp'), may hold values from -2 to 8
- w_out: bfloat16 [1536, 1536], P('tp', 'fsdp'), may hold values from -0.625 to 0.625
- w_gate_up: bfloat16 [1536, 2, 4096], P('fsdp', None, 'tp'), may hold values from -0.15625 to 0.15625
- w_down: bfloat16 [4096, 1536], P('tp', 'fsdp'), may hold values from -0.09375 to 0.09375
- gain_attn: bfloat16 [1536], replicated, may hold values from 0.5 to 1.5
- gain_ffn: bfloat16 [1536], replicated, may hold values from 0.5 to 1.5
- a_qkv: bfloat16 [8, 1536, 16], replicated, may hold values from -0.15625 to 0.15625
- b_qkv: bfloat16 [8, 16, 3, 1536], replicated, may hold values from -1.5 to 1.5
- a_out: bfloat16 [8, 1536, 16], replicated, may hold values from -0.625 to 0.625
- b_out: bfloat16 [8, 16, 1536], replicated, may hold values from -1.5 to 1.5
- a_gate_up: bfloat16 [8, 1536, 16], replicated, may hold values from -0.15625 to 0.15625
- b_gate_up: bfloat16 [8, 16, 2, 4096], replicated, may hold values from -1.5 to 1.5
- a_down: bfloat16 [8, 4096, 16], replicated, may hold values from -0.09375 to 0.09375
- b_down: bfloat16 [8, 16, 1536], replicated, may hold values from -1.5 to 1.5
- cotangent: bfloat16 [4, 2048, 1536], P('fsdp', 'ctx'), may hold values from -6 to 6
Outputs:
- block_output: bfloat16 [4, 2048, 1536], P('fsdp', 'ctx')
- grad_tokens: float32 [4, 2048, 1536], P('fsdp', 'ctx')
- grad_a_qkv: float32 [8, 1536, 16], P(None, ('fsdp', 'ctx', 'tp'))
- grad_b_qkv: float32 [8, 16, 3, 1536], P(None, None, None, ('fsdp', 'ctx', 'tp'))
- grad_a_out: float32 [8, 1536, 16], P(None, ('fsdp', 'ctx', 'tp'))
- grad_b_out: float32 [8, 16, 1536], P(None, None, ('fsdp', 'ctx', 'tp'))
- grad_a_gate_up: float32 [8, 1536, 16], P(None, ('fsdp', 'ctx', 'tp'))
- grad_b_gate_up: float32 [8, 16, 2, 4096], P(None, None, None, ('fsdp', 'ctx', 'tp'))
- grad_a_down: float32 [8, 4096, 16], P(None, ('fsdp', 'ctx', 'tp'))
- grad_b_down: float32 [8, 16, 1536], P(None, None, ('fsdp', 'ctx', 'tp'))
Inputs may be any that keep to these rules, and one draw needn't show every extreme that they name: `segments`: document numbers never fall along a sequence; every document of 0 to 7 is present with 1 to 800 tokens, and one has exactly 800.
All inputs are finite; a program needn't handle non-finite values.
Results may differ from a plain program's by a relative error of at most 0.01575.
The roundings to bfloat16 on the way count: a program that leaves them out, or rounds other values in their place, can miss the bound.
Values may be sent and summed in bfloat16 or wider, within the bound.
No kernel may reach another device: no remote copies, remote signals or barrier semaphores. Data moves between devices by JAX's collectives and lax.ppermute only.
A program may use at most 576 MiB of HBM per device.

v0:
```python
import jax
import jax.numpy as jnp
from jax import lax
from jax.sharding import PartitionSpec as P

HD = 64


def carried_in(array, axis, combine, identity, reverse):
    size, index = (lax.axis_size(axis), lax.axis_index(axis))
    everything = jax.tree.map(lambda part: lax.all_gather(part, axis), array)
    start = jax.tree.map(
        lambda part, zero: jnp.broadcast_to(jnp.asarray(zero, part.dtype), part.shape),
        array,
        identity,
    )

    def hop(k, before):
        at = size - 1 - k if reverse else k
        reached = at > index if reverse else at < index
        new = combine(before, jax.tree.map(lambda part: part[at], everything))
        return jax.tree.map(lambda a, b: jnp.where(reached, a, b), new, before)

    return lax.fori_loop(0, size, hop, start)


def rms_norm(values, gain_vec):
    return values * lax.rsqrt(jnp.mean(values * values, axis=-1, keepdims=True) + 1e-05) * gain_vec


def rms_back(values, gain_vec, incoming):
    factor = lax.rsqrt(jnp.mean(values * values, axis=-1, keepdims=True) + 1e-05)
    scaled = incoming * gain_vec
    return factor * scaled - values * factor**3 * jnp.mean(values * scaled, axis=-1, keepdims=True)


def seg_combine(earlier, subsequent):
    early_first, early_last, early_tail = earlier
    late_first, late_last, late_tail = subsequent
    first_seg = jnp.where(early_first < 0, late_first, early_first)
    last_seg = jnp.where(late_last < 0, early_last, late_last)
    joined = (late_first == late_last) & (early_last == late_first)
    tail_sum = jnp.where(late_last < 0, early_tail, late_tail + jnp.where(joined, early_tail, 0.0))
    return (first_seg, last_seg, tail_sum)


def choose(onehot, table):
    return jnp.einsum("sa,a...->s...", onehot, table, preferred_element_type=jnp.float32).astype(
        jnp.bfloat16
    )


def spread(onehot, grad_sel):
    return jnp.einsum(
        "sa,s...->a...",
        onehot.astype(jnp.float32),
        grad_sel,
        precision=lax.Precision.HIGHEST,
        preferred_element_type=jnp.float32,
    )


def widen(part, full_shape, axis_num, offset):
    blank_full = jnp.zeros(full_shape, jnp.float32)
    return lax.dynamic_update_slice_in_dim(blank_full, part, offset, axis_num)


def to_heads(values, head_size):
    seq_count, pos_count, col_count = values.shape
    return values.reshape(seq_count, pos_count, col_count // head_size, head_size).transpose(
        2, 0, 1, 3
    )


def from_heads(values):
    head_count, seq_count, pos_count, size_count = values.shape
    return values.transpose(1, 2, 0, 3).reshape(seq_count, pos_count, head_count * size_count)


def head_scores(queries, key_part, gate_query, gate_key, allowed):
    scores = jnp.einsum(
        "sqd,skd->sqk", queries, key_part, preferred_element_type=jnp.float32
    ) * HD ** (-0.5)
    scores = scores + gate_query[:, :, None] - gate_key[:, None, :]
    return jnp.where(allowed, scores, -1e30)


def head_forward(head_item, allowed):
    queries, key_part, value_part, gate_query, gate_key = head_item
    scores = head_scores(queries, key_part, gate_query, gate_key, allowed)
    top_score = jnp.max(scores, axis=-1, keepdims=True)
    weights = jnp.exp(scores - top_score)
    row_total = jnp.sum(weights, axis=-1, keepdims=True)
    weights = weights / row_total
    mixed_out = jnp.einsum(
        "sqk,skd->sqd", weights.astype(jnp.bfloat16), value_part, preferred_element_type=jnp.float32
    )
    return (mixed_out, (top_score + jnp.log(row_total))[:, :, 0])


def head_backward(head_item, allowed):
    queries, key_part, value_part, gate_query, gate_key, log_total, grad_out = head_item
    scores = head_scores(queries, key_part, gate_query, gate_key, allowed)
    weights = jnp.exp(scores - log_total[:, :, None])
    grad_weights = jnp.einsum(
        "sqd,skd->sqk", grad_out, value_part, preferred_element_type=jnp.float32
    )
    inner_sum = jnp.sum(weights * grad_weights, axis=-1, keepdims=True)
    grad_scores = (weights * (grad_weights - inner_sum)).astype(jnp.bfloat16)
    grad_query = jnp.einsum(
        "sqk,skd->sqd", grad_scores, key_part, preferred_element_type=jnp.float32
    ) * HD ** (-0.5)
    grad_key = jnp.einsum(
        "sqk,sqd->skd", grad_scores, queries, preferred_element_type=jnp.float32
    ) * HD ** (-0.5)
    grad_value = jnp.einsum(
        "sqk,sqd->skd", weights.astype(jnp.bfloat16), grad_out, preferred_element_type=jnp.float32
    )
    score_sums = grad_scores.astype(jnp.float32)
    return (
        grad_query,
        grad_key,
        grad_value,
        jnp.sum(score_sums, axis=2),
        -jnp.sum(score_sums, axis=1),
    )


def body(
    tokens,
    segments,
    adapter_index,
    w_qkv,
    w_forget,
    forget_bias,
    w_out,
    w_gate_up,
    w_down,
    gain_attn,
    gain_ffn,
    a_qkv,
    b_qkv,
    a_out,
    b_out,
    a_gate_up,
    b_gate_up,
    a_down,
    b_down,
    cotangent,
):
    seq_count, local_len, model_width = tokens.shape
    tok_rows = seq_count * local_len
    head_cols = w_qkv.shape[2]
    local_heads = w_forget.shape[1]
    head_size = head_cols // local_heads
    unit_cols = w_gate_up.shape[2]
    tp_rank = lax.axis_index("tp")
    full_len = local_len * lax.axis_size("ctx")
    query_pos = lax.axis_index("ctx") * local_len + jnp.arange(local_len)
    key_pos = jnp.arange(full_len)
    onehot = (adapter_index[:, None] == jnp.arange(a_qkv.shape[0])[None, :]).astype(jnp.bfloat16)
    qkv_a = choose(onehot, a_qkv)
    qkv_b = choose(onehot, lax.dynamic_slice_in_dim(b_qkv, tp_rank * head_cols, head_cols, 3))
    out_a = choose(onehot, lax.dynamic_slice_in_dim(a_out, tp_rank * head_cols, head_cols, 1))
    out_b = choose(onehot, b_out)
    ffn_a = choose(onehot, a_gate_up)
    ffn_b = choose(onehot, lax.dynamic_slice_in_dim(b_gate_up, tp_rank * unit_cols, unit_cols, 3))
    down_a = choose(onehot, lax.dynamic_slice_in_dim(a_down, tp_rank * unit_cols, unit_cols, 1))
    down_b = choose(onehot, b_down)
    seg_float = segments.astype(jnp.float32)
    seg_col = seg_float[:, :, None]
    x_float = tokens.astype(jnp.float32)
    gain_one = gain_attn.astype(jnp.float32)
    gain_two = gain_ffn.astype(jnp.float32)
    bias_float = forget_bias.astype(jnp.float32)
    blank = (
        -jnp.ones((seq_count, 1), jnp.float32),
        -jnp.ones((seq_count, 1), jnp.float32),
        jnp.zeros((seq_count, local_heads), jnp.float32),
    )

    def attn_forward():
        qkv_w, forget_w, out_w = (
            lax.all_gather(w_qkv, "fsdp", axis=0, tiled=True),
            lax.all_gather(w_forget, "fsdp", axis=0, tiled=True),
            lax.all_gather(w_out, "fsdp", axis=1, tiled=True),
        )
        normed = rms_norm(x_float, gain_one).astype(jnp.bfloat16)
        flat_normed = normed.reshape(tok_rows, model_width)
        low_qkv = jnp.einsum(
            "std,sdr->str", normed, qkv_a, preferred_element_type=jnp.float32
        ).astype(jnp.bfloat16)
        projected = jnp.dot(
            flat_normed,
            qkv_w.reshape(model_width, 3 * head_cols),
            preferred_element_type=jnp.float32,
        )
        projected = projected.reshape(seq_count, local_len, 3, head_cols)
        projected = projected + jnp.einsum(
            "str,srch->stch", low_qkv, qkv_b, preferred_element_type=jnp.float32
        )
        proj_low = projected.astype(jnp.bfloat16)
        logits = (
            jnp.dot(flat_normed, forget_w, preferred_element_type=jnp.float32).reshape(
                seq_count, local_len, local_heads
            )
            + bias_float
        )
        log_forget = jax.nn.log_sigmoid(logits)
        local_gates = lax.associative_scan(seg_combine, (seg_col, seg_col, log_forget), axis=1)[2]
        summary = (seg_float[:, :1], seg_float[:, -1:], local_gates[:, -1, :])
        incoming = carried_in(summary, "ctx", seg_combine, blank, False)
        gates = local_gates + jnp.where(
            seg_col == incoming[1][:, :, None], incoming[2][:, None, :], 0.0
        )
        key_all, value_all = (
            lax.all_gather(proj_low[:, :, 1], "ctx", axis=1, tiled=True),
            lax.all_gather(proj_low[:, :, 2], "ctx", axis=1, tiled=True),
        )
        gate_all, seg_all = (
            lax.all_gather(gates, "ctx", axis=1, tiled=True),
            lax.all_gather(seg_float, "ctx", axis=1, tiled=True),
        )
        allowed = (seg_all[:, None, :] == seg_col) & (
            key_pos[None, None, :] <= query_pos[None, :, None]
        )
        mixed, log_total = lax.map(
            lambda head_item: head_forward(head_item, allowed),
            (
                to_heads(proj_low[:, :, 0], head_size),
                to_heads(key_all, head_size),
                to_heads(value_all, head_size),
                gates.transpose(2, 0, 1),
                gate_all.transpose(2, 0, 1),
            ),
        )
        mixed_low = from_heads(mixed).astype(jnp.bfloat16)
        out_part = jnp.dot(
            mixed_low.reshape(tok_rows, head_cols), out_w, preferred_element_type=jnp.float32
        )
        low_part = jnp.einsum("stc,scr->str", mixed_low, out_a, preferred_element_type=jnp.float32)
        attended, low_out = lax.psum((out_part, low_part), "tp")
        low_out_b = low_out.astype(jnp.bfloat16)
        attended = attended.reshape(seq_count, local_len, model_width) + jnp.einsum(
            "str,srd->std", low_out_b, out_b, preferred_element_type=jnp.float32
        )
        hidden_in = x_float + attended
        return (
            qkv_w,
            forget_w,
            out_w,
            normed,
            low_qkv,
            proj_low,
            logits,
            key_all,
            value_all,
            gates,
            gate_all,
            allowed,
            log_total,
            mixed_low,
            low_out_b,
            hidden_in,
        )

    def ffn_forward(hidden_in):
        gate_up_w, down_w = (
            lax.all_gather(w_gate_up, "fsdp", axis=0, tiled=True),
            lax.all_gather(w_down, "fsdp", axis=1, tiled=True),
        )
        normed_ffn = rms_norm(hidden_in, gain_two).astype(jnp.bfloat16)
        low_ffn = jnp.einsum(
            "std,sdr->str", normed_ffn, ffn_a, preferred_element_type=jnp.float32
        ).astype(jnp.bfloat16)
        both = jnp.dot(
            normed_ffn.reshape(tok_rows, model_width),
            gate_up_w.reshape(model_width, 2 * unit_cols),
            preferred_element_type=jnp.float32,
        )
        both = both.reshape(seq_count, local_len, 2, unit_cols) + jnp.einsum(
            "str,srcf->stcf", low_ffn, ffn_b, preferred_element_type=jnp.float32
        )
        gate_val = both[:, :, 0]
        up_val = both[:, :, 1]
        units = (jax.nn.silu(gate_val) * up_val).astype(jnp.bfloat16)
        return (gate_up_w, down_w, normed_ffn, low_ffn, gate_val, up_val, units)

    attn_state = attn_forward()
    ffn_state = ffn_forward(attn_state[15])
    units = ffn_state[6]
    down_part = jnp.dot(
        units.reshape(tok_rows, unit_cols), ffn_state[1], preferred_element_type=jnp.float32
    )
    low_down_part = jnp.einsum("stf,sfr->str", units, down_a, preferred_element_type=jnp.float32)
    ffn_out, low_down = lax.psum((down_part, low_down_part), "tp")
    low_down_b = low_down.astype(jnp.bfloat16)
    block_output = (
        attn_state[15]
        + ffn_out.reshape(seq_count, local_len, model_width)
        + jnp.einsum("str,srd->std", low_down_b, down_b, preferred_element_type=jnp.float32)
    )
    attn_state = attn_forward()
    ffn_state = ffn_forward(attn_state[15])
    (
        qkv_w,
        forget_w,
        out_w,
        normed,
        low_qkv,
        proj_low,
        logits,
        key_all,
        value_all,
        gates,
        gate_all,
        allowed,
        log_total,
        mixed_low,
        low_out_b,
        hidden_in,
    ) = attn_state
    gate_up_w, down_w, normed_ffn, low_ffn, gate_val, up_val, units = ffn_state
    grad_low_down = jnp.einsum(
        "std,srd->str", cotangent, down_b, preferred_element_type=jnp.float32
    ).astype(jnp.bfloat16)
    grad_down_b = jnp.einsum(
        "str,std->srd", low_down_b, cotangent, preferred_element_type=jnp.float32
    )
    grad_units = jnp.dot(
        cotangent.reshape(tok_rows, model_width), down_w.T, preferred_element_type=jnp.float32
    ).reshape(seq_count, local_len, unit_cols)
    grad_units = grad_units + jnp.einsum(
        "str,sfr->stf", grad_low_down, down_a, preferred_element_type=jnp.float32
    )
    grad_down_a = jnp.einsum(
        "stf,str->sfr", units, grad_low_down, preferred_element_type=jnp.float32
    )
    sigmoid_gate = jax.nn.sigmoid(gate_val)
    grad_gate = grad_units * up_val * sigmoid_gate * (1.0 + gate_val * (1.0 - sigmoid_gate))
    grad_up = grad_units * gate_val * sigmoid_gate
    grad_both = jnp.stack([grad_gate, grad_up], axis=2).astype(jnp.bfloat16)
    normed_part = jnp.dot(
        grad_both.reshape(tok_rows, 2 * unit_cols),
        gate_up_w.reshape(model_width, 2 * unit_cols).T,
        preferred_element_type=jnp.float32,
    )
    low_ffn_part = jnp.einsum(
        "stcf,srcf->str", grad_both, ffn_b, preferred_element_type=jnp.float32
    )
    grad_ffn_b = jnp.einsum(
        "str,stcf->srcf", low_ffn, grad_both, preferred_element_type=jnp.float32
    )
    grad_normed_ffn, grad_low_ffn = lax.psum((normed_part, low_ffn_part), "tp")
    grad_low_ffn_b = grad_low_ffn.astype(jnp.bfloat16)
    grad_normed_ffn = grad_normed_ffn.reshape(seq_count, local_len, model_width) + jnp.einsum(
        "str,sdr->std", grad_low_ffn_b, ffn_a, preferred_element_type=jnp.float32
    )
    grad_ffn_a = jnp.einsum(
        "std,str->sdr", normed_ffn, grad_low_ffn_b, preferred_element_type=jnp.float32
    )
    grad_hidden = cotangent.astype(jnp.float32) + rms_back(hidden_in, gain_two, grad_normed_ffn)
    grad_hidden_b = grad_hidden.astype(jnp.bfloat16)
    grad_low_out = jnp.einsum(
        "std,srd->str", grad_hidden_b, out_b, preferred_element_type=jnp.float32
    ).astype(jnp.bfloat16)
    grad_out_b = jnp.einsum(
        "str,std->srd", low_out_b, grad_hidden_b, preferred_element_type=jnp.float32
    )
    grad_mixed = jnp.dot(
        grad_hidden_b.reshape(tok_rows, model_width), out_w.T, preferred_element_type=jnp.float32
    ).reshape(seq_count, local_len, head_cols)
    grad_mixed = (
        grad_mixed
        + jnp.einsum("str,scr->stc", grad_low_out, out_a, preferred_element_type=jnp.float32)
    ).astype(jnp.bfloat16)
    grad_out_a = jnp.einsum(
        "stc,str->scr", mixed_low, grad_low_out, preferred_element_type=jnp.float32
    )
    grad_query, grad_key, grad_value, grad_gate_q, grad_gate_k = lax.map(
        lambda head_item: head_backward(head_item, allowed),
        (
            to_heads(proj_low[:, :, 0], head_size),
            to_heads(key_all, head_size),
            to_heads(value_all, head_size),
            gates.transpose(2, 0, 1),
            gate_all.transpose(2, 0, 1),
            log_total,
            to_heads(grad_mixed, head_size),
        ),
    )
    own_key, own_value, own_gate = (
        lax.psum_scatter(from_heads(grad_key), "ctx", scatter_dimension=1, tiled=True),
        lax.psum_scatter(from_heads(grad_value), "ctx", scatter_dimension=1, tiled=True),
        lax.psum_scatter(grad_gate_k.transpose(1, 2, 0), "ctx", scatter_dimension=1, tiled=True),
    )
    grad_gates = grad_gate_q.transpose(1, 2, 0) + own_gate
    local_back = lax.associative_scan(
        seg_combine, (seg_col, seg_col, grad_gates), reverse=True, axis=1
    )[2]
    summary_back = (seg_float[:, -1:], seg_float[:, :1], local_back[:, 0, :])
    incoming_back = carried_in(summary_back, "ctx", seg_combine, blank, True)
    grad_log_forget = local_back + jnp.where(
        seg_col == incoming_back[1][:, :, None], incoming_back[2][:, None, :], 0.0
    )
    grad_logits = (grad_log_forget * jax.nn.sigmoid(-logits)).astype(jnp.bfloat16)
    grad_proj = jnp.stack([from_heads(grad_query), own_key, own_value], axis=2).astype(jnp.bfloat16)
    normed_back = jnp.dot(
        grad_proj.reshape(tok_rows, 3 * head_cols),
        qkv_w.reshape(model_width, 3 * head_cols).T,
        preferred_element_type=jnp.float32,
    )
    normed_back = normed_back + jnp.dot(
        grad_logits.reshape(tok_rows, local_heads), forget_w.T, preferred_element_type=jnp.float32
    )
    low_qkv_part = jnp.einsum(
        "stch,srch->str", grad_proj, qkv_b, preferred_element_type=jnp.float32
    )
    grad_qkv_b = jnp.einsum(
        "str,stch->srch", low_qkv, grad_proj, preferred_element_type=jnp.float32
    )
    grad_normed, grad_low_qkv = lax.psum((normed_back, low_qkv_part), "tp")
    grad_low_qkv_b = grad_low_qkv.astype(jnp.bfloat16)
    grad_normed = grad_normed.reshape(seq_count, local_len, model_width) + jnp.einsum(
        "str,sdr->std", grad_low_qkv_b, qkv_a, preferred_element_type=jnp.float32
    )
    grad_qkv_a = jnp.einsum(
        "std,str->sdr", normed, grad_low_qkv_b, preferred_element_type=jnp.float32
    )
    grad_tokens = grad_hidden + rms_back(x_float, gain_one, grad_normed)
    keep_first = (tp_rank == 0).astype(jnp.float32)
    pieces = (
        grad_qkv_a * keep_first,
        widen(grad_qkv_b, (seq_count,) + b_qkv.shape[1:], 3, tp_rank * head_cols),
        widen(grad_out_a, (seq_count,) + a_out.shape[1:], 1, tp_rank * head_cols),
        grad_out_b * keep_first,
        grad_ffn_a * keep_first,
        widen(grad_ffn_b, (seq_count,) + b_gate_up.shape[1:], 3, tp_rank * unit_cols),
        widen(grad_down_a, (seq_count,) + a_down.shape[1:], 1, tp_rank * unit_cols),
        grad_down_b * keep_first,
    )
    summed = (
        lax.psum_scatter(
            spread(onehot, pieces[0]), ("fsdp", "ctx", "tp"), scatter_dimension=1, tiled=True
        ),
        lax.psum_scatter(
            spread(onehot, pieces[1]), ("fsdp", "ctx", "tp"), scatter_dimension=3, tiled=True
        ),
        lax.psum_scatter(
            spread(onehot, pieces[2]), ("fsdp", "ctx", "tp"), scatter_dimension=1, tiled=True
        ),
        lax.psum_scatter(
            spread(onehot, pieces[3]), ("fsdp", "ctx", "tp"), scatter_dimension=2, tiled=True
        ),
        lax.psum_scatter(
            spread(onehot, pieces[4]), ("fsdp", "ctx", "tp"), scatter_dimension=1, tiled=True
        ),
        lax.psum_scatter(
            spread(onehot, pieces[5]), ("fsdp", "ctx", "tp"), scatter_dimension=3, tiled=True
        ),
        lax.psum_scatter(
            spread(onehot, pieces[6]), ("fsdp", "ctx", "tp"), scatter_dimension=1, tiled=True
        ),
        lax.psum_scatter(
            spread(onehot, pieces[7]), ("fsdp", "ctx", "tp"), scatter_dimension=2, tiled=True
        ),
    )
    return (
        block_output.astype(jnp.bfloat16),
        grad_tokens,
        summed[0],
        summed[1],
        summed[2],
        summed[3],
        summed[4],
        summed[5],
        summed[6],
        summed[7],
    )


def solution(mesh):
    in_specs = (
        P("fsdp", "ctx", None),
        P("fsdp", "ctx"),
        P("fsdp"),
        P("fsdp", None, "tp"),
        P("fsdp", "tp"),
        P("tp"),
        P("tp", "fsdp"),
        P("fsdp", None, "tp"),
        P("tp", "fsdp"),
        P(),
        P(),
        P(),
        P(),
        P(),
        P(),
        P(),
        P(),
        P(),
        P(),
        P("fsdp", "ctx", None),
    )
    out_specs = (
        P("fsdp", "ctx", None),
        P("fsdp", "ctx", None),
        P(None, ("fsdp", "ctx", "tp"), None),
        P(None, None, None, ("fsdp", "ctx", "tp")),
        P(None, ("fsdp", "ctx", "tp"), None),
        P(None, None, ("fsdp", "ctx", "tp")),
        P(None, ("fsdp", "ctx", "tp"), None),
        P(None, None, None, ("fsdp", "ctx", "tp")),
        P(None, ("fsdp", "ctx", "tp"), None),
        P(None, None, ("fsdp", "ctx", "tp")),
    )
    return jax.shard_map(body, mesh=mesh, in_specs=in_specs, out_specs=out_specs, check_vma=False)
```

profile of v0, /device:TPU:0, one launch (start us, length us, event | category | flops | bytes accessed | tf_op | source)
XLA Modules:
  0.0 2340.1 jit_solution(6752047072097069952)
XLA Ops:
  18.6 46.4 %all-gather.11.cloned.1.call-done = bf16[1536,3,768]{0,2,1:T(8,128)(2,1)} async-done(((bf16[384,3,768]{0,2,1:T(8,128)(2,1)}), bf16[1536,3,768]{0,2,1:T(8,128)(2,1)}) %all-gather.11.cloned.1.call-update) | async-done | bytes 7077904 | tf_op jit(solution)/shard_map/all_gather | solution.py:184
  84.6 12.7 all_gather.30
  150.5 15.2 while.86
  165.8 14.3 all_gather.72
  215.1 73.2 %while.84 = (s32[]{:T(128)}, bf16[12,1,512,64]{2,3,1,0:T(8,128)(2,1)S(1)}, f32[12,1,512]{2,1,0:T(1,128)}, bf16[12,1,512,64]{3,2,1,0:T(8,128)(2,1)}, bf16[12,1,20...) while((s32[]{:T(128)}, ...), condition=%wide.region_15.16_spmd.clone, body=%wide.region_12.15_spmd.clone.sunk | while | flops 282066432 | bytes 13959305 | solution.py:227
  325.7 75.2 %while.83 = (s32[]{:T(128)}, bf16[12,1,512,64]{2,3,1,0:T(8,128)(2,1)S(1)}, bf16[12,1,512,64]{3,2,1,0:T(8,128)(2,1)}, bf16[12,1,2048,64]{3,2,1,0:T(8,128)(2,1)}, ...) while((s32[]{:T(128)}, ...), condition=%wide.region_6.7_spmd.clone, body=%wide.region_3.6_spmd.clone.sunk | while | flops 282065920 | bytes 13949053 | solution.py:227
  410.9 51.7 %all-gather.15.cloned.1.call-done = bf16[1536,2,2048]{2,1,0:T(2,128)(2,1)} async-done(((bf16[384,2,2048]{2,1,0:T(2,128)(2,1)}), bf16[1536,2,2048]{2,1,0:T(2,128)(2,1)}) %all-gather.15.cloned.1.call-update) | async-done | bytes 12582928 | tf_op jit(solution)/shard_map/all_gather | solution.py:269
  462.6 13.3 copy.296
  475.9 16.6 copy.158
  517.8 12.3 fusion.253
  544.0 141.1 %all-reduce.83.cloned.1.call-done = (f32[512,1536]{1,0:T(8,128)}, f32[512,1536]{1,0:T(8,128)}) async-done(((f32[512,1536]{1,0:T(8,128)}, f32[512,1536]{1,0:T(8,128)}), (f32[512,1536]{1,0:T(8,128)}, f32[512,1536]{1,0:T(8,128)})) %all-reduce.83.cloned.1.call-update) | async-done | bytes 6291472 | tf_op jit(solution)/shard_map/psum | solution.py:242
  696.3 226.4 %while.85 = (s32[]{:T(128)}, bf16[12,1,512,64]{2,3,1,0:T(8,128)(2,1)S(1)}, f32[12,1,2048,64]{2,3,1,0:T(8,128)}, f32[12,1,2048,64]{2,3,1,0:T(8,128)}, f32[12,1,51...) while((s32[]{:T(128)}, ...), condition=%wide.region_26.27_spmd.clone, body=%wide.region_22.26_spmd.clone.sunk | while | flops 689077248 | bytes 51485912 | solution.py:380
  974.0 129.4 %copy.214 = f32[8,16,2,4096]{2,1,0,3:T(8,128)} copy(f32[8,16,2,4096]{3,2,1,0:T(2,128)} %broadcast_multiply_fusion) | data formatting | bytes 8388608
  1103.4 184.2 %reshape.1300 = f32[4096,256]{1,0:T(8,128)} reshape(f32[4096,8,16,2]{3,2,1,0:T(8,128)} %bitcast.236) | data formatting | bytes 8388608
  1417.8 20.7 copy.206
  1438.5 25.8 %reshape.1292 = f32[1536,384]{1,0:T(8,128)} reshape(f32[1536,8,3,16]{3,2,1,0:T(4,128)} %bitcast.764) | data formatting | bytes 4718592
  1475.0 17.8 while.87
  1536.0 95.7 %reduce-scatter.46.cloned.1.call-done = f32[48,128]{1,0:T(8,128)} async-done(((f32[1536,128]{1,0:T(8,128)}), f32[48,128]{1,0:T(8,128)}) %reduce-scatter.46.cloned.1.call-update) | async-done | bytes 24592
  1633.4 98.8 %reduce-scatter.38.cloned.1.call-done = f32[48,128]{1,0:T(8,128)} async-done(((f32[1536,128]{1,0:T(8,128)}), f32[48,128]{1,0:T(8,128)}) %reduce-scatter.38.cloned.1.call-update) | async-done | bytes 24592
  1733.8 98.7 %reduce-scatter.34.cloned.1.call-done = f32[48,128]{1,0:T(8,128)} async-done(((f32[1536,128]{1,0:T(8,128)}), f32[48,128]{1,0:T(8,128)}) %reduce-scatter.34.cloned.1.call-update) | async-done | bytes 24592
  1834.0 98.7 %reduce-scatter.40.cloned.1.call-done = f32[48,128]{1,0:T(8,128)} async-done(((f32[1536,128]{1,0:T(8,128)}), f32[48,128]{1,0:T(8,128)}) %reduce-scatter.40.cloned.1.call-update) | async-done | bytes 24592
  1934.4 102.5 %reduce-scatter.36.cloned.1.call-done = f32[48,384]{1,0:T(8,128)} async-done(((f32[1536,384]{1,0:T(8,128)}), f32[48,384]{1,0:T(8,128)}) %reduce-scatter.36.cloned.1.call-update) | async-done | bytes 73744
  2039.5 152.5 %all-reduce.81.cloned.1.call-done = (f32[1,512,1536]{2,1,0:T(8,128)}, f32[512,1536]{1,0:T(8,128)}) async-done(((f32[1,512,1536]{2,1,0:T(8,128)}, f32[512,1536]{1,0:T(8,128)}), (f32[1,512,1536]{2,1,0:T(8,128)}, f32[512,1536]{1,0:T(8,128)})) %all-reduce.81.cloned.1.call-update) | async-done | bytes 6291472 | tf_op jit(solution)/shard_map/psum | solution.py:296
  2201.1 131.7 %reduce-scatter.32.cloned.1.call-done = f32[8,128,16]{1,2,0:T(8,128)} async-done(((f32[8,4096,16]{1,2,0:T(8,128)}), f32[8,128,16]{1,2,0:T(8,128)}) %reduce-scatter.32.cloned.1.call-update) | async-done | bytes 65552 | tf_op jit(solution)/shard_map/reduce_scatter | solution.py:461
  (1169 shorter events, 832.7 us)
Async XLA Ops:
  7.2 295.4 %copy-start = (bf16[8,16,2,4096]{3,2,1,0:T(2,128)(2,1)S(1)}, bf16[8,16,2,4096]{3,2,1,0:T(2,128)(2,1)}, u32[]{:S(2)}) copy-start(bf16[8,16,2,4096]{3,2,1,0:T(2,128)(2,1)} %param.46) | copy-start | bytes 6291460
  7.2 57.8 %all-gather.11.cloned.1.call-start = ((), (), s32[]{:S(2)}) async-start(), calls=%async_computation.11 | async-start | bytes 8847360 | tf_op jit(solution)/shard_map/all_gather | solution.py:184
  11.3 172.6 %all-gather.19.cloned.1.call-start = ((), (), s32[]{:S(2)}) async-start(), calls=%async_computation.20 | async-start | bytes 3932160 | tf_op jit(solution)/shard_map/all_gather | solution.py:217
  74.1 129.7 %all-gather.21.cloned.1.call-start = ((), (), s32[]{:S(2)}) async-start(), calls=%async_computation.21 | async-start | bytes 3932160 | tf_op jit(solution)/shard_map/all_gather | solution.py:218
  74.8 213.5 %all-gather.13.cloned.1.call-start = ((), (), s32[]{:S(2)}) async-start(), calls=%async_computation.12 | async-start | bytes 2949120 | tf_op jit(solution)/shard_map/all_gather | solution.py:186
  75.4 233.0 %all-gather.17.cloned.1.call-start = ((), (), s32[]{:S(2)}) async-start(), calls=%async_computation.14 | async-start | bytes 7864320 | tf_op jit(solution)/shard_map/all_gather | solution.py:270
  76.0 329.7 %all-reduce.79.cloned.1.call-start = ((), (), s32[]{:S(2)}) async-start(), calls=%async_computation.15 | async-start | bytes 6291456 | tf_op jit(solution)/shard_map/psum | solution.py:242
  293.5 169.1 %all-gather.15.cloned.1.call-start = ((), (), s32[]{:S(2)}) async-start(), calls=%async_computation.13 | async-start | bytes 15728640 | tf_op jit(solution)/shard_map/all_gather | solution.py:269
  294.2 391.0 %all-reduce.83.cloned.1.call-start = ((), (), s32[]{:S(2)}) async-start(), calls=%async_computation.30 | async-start | bytes 12582912 | tf_op jit(solution)/shard_map/psum | solution.py:242
  294.7 390.5 %copy-start.58 = (f32[1536]{0:T(1024)}, f32[1536]{0:T(1024)S(1)}, u32[]{:S(2)}) copy-start(f32[1536]{0:T(1024)S(1)} %convert_element_type.260) | copy-start | bytes 18436
  298.2 387.0 %copy-start.24 = (bf16[1,1536,16]{2,1,0:T(8,128)(2,1)}, bf16[1,1536,16]{2,1,0:T(8,128)(2,1)S(1)}, u32[]{:S(2)}) copy-start(bf16[1,1536,16]{2,1,0:T(8,128)(2,1)S(1)} %copy.196) | copy-start | bytes 147460
  530.1 802.9 %reduce-scatter.30.cloned.1.call-start = ((), (), s32[]{:S(2)}) async-start(), calls=%async_computation.18 | async-start | bytes 163840 | tf_op jit(solution)/shard_map/reduce_scatter | solution.py:395
  922.7 413.1 %reduce-scatter.26.cloned.1.call-start = ((), (), s32[]{:S(2)}) async-start(), calls=%async_computation.16 | async-start | bytes 7864320 | tf_op jit(solution)/shard_map/reduce_scatter | solution.py:393
  929.6 409.0 %reduce-scatter.28.cloned.1.call-start = ((), (), s32[]{:S(2)}) async-start(), calls=%async_computation.17 | async-start | bytes 7864320 | tf_op jit(solution)/shard_map/reduce_scatter | solution.py:394
  936.2 580.4 %reduce-scatter.44.cloned.1.call-start = ((), (), s32[]{:S(2)}) async-start(), calls=%async_computation.27 | async-start | bytes 4325376
  1287.8 246.6 %reduce-scatter.42.cloned.1.call-start = ((), (), s32[]{:S(2)}) async-start(), calls=%async_computation.26 | async-start | bytes 811008
  1365.1 266.7 %reduce-scatter.46.cloned.1.call-start = ((), (), s32[]{:S(2)}) async-start(), calls=%async_computation.28 | async-start | bytes 811008
  1379.0 353.1 %reduce-scatter.38.cloned.1.call-start = ((), (), s32[]{:S(2)}) async-start(), calls=%async_computation.24 | async-start | bytes 811008
  1390.0 442.4 %reduce-scatter.34.cloned.1.call-start = ((), (), s32[]{:S(2)}) async-start(), calls=%async_computation.22 | async-start | bytes 811008
  1401.0 531.7 %reduce-scatter.40.cloned.1.call-start = ((), (), s32[]{:S(2)}) async-start(), calls=%async_computation.25 | async-start | bytes 811008
  1413.3 623.6 %reduce-scatter.36.cloned.1.call-start = ((), (), s32[]{:S(2)}) async-start(), calls=%async_computation.23 | async-start | bytes 2433024
  1464.3 727.8 %all-reduce.81.cloned.1.call-start = ((), (), s32[]{:S(2)}) async-start(), calls=%async_computation.29 | async-start | bytes 12582912 | tf_op jit(solution)/shard_map/psum | solution.py:296
  1509.6 823.3 %reduce-scatter.32.cloned.1.call-start = ((), (), s32[]{:S(2)}) async-start(), calls=%async_computation.19 | async-start | bytes 2162688 | tf_op jit(solution)/shard_map/reduce_scatter | solution.py:461
  1534.4 657.7 %copy-start.32 = (bf16[1,1536,16]{2,1,0:T(8,128)(2,1)S(1)}, bf16[1,1536,16]{2,1,0:T(8,128)(2,1)}, u32[]{:S(2)}) copy-start(bf16[1,1536,16]{2,1,0:T(8,128)(2,1)} %copy-done.31) | copy-start | bytes 147460
  (142 other events, 2062.1 us)
Sparse Core Ops, SparseCore 0:
  11.4 53.5 all-gather.10
  74.2 63.6 all-gather.18
  139.5 64.2 all-gather.20
  205.2 22.7 all-gather.12
  229.4 46.2 all-gather.16
  293.6 85.1 all-reduce.78
  380.4 82.1 all-gather.14
  530.2 154.8 all-reduce.82
  922.8 19.2 reduce-scatter.29
  944.3 108.9 reduce-scatter.25
  1055.7 111.2 reduce-scatter.27
  1287.8 144.9 reduce-scatter.43
  1438.7 92.7 reduce-scatter.41
  1537.2 94.4 reduce-scatter.45
  1637.5 94.5 reduce-scatter.37
  1737.9 94.4 reduce-scatter.33
  1838.2 94.5 reduce-scatter.39
  1938.8 98.0 reduce-scatter.35
  2039.4 152.5 all-reduce.80
  2194.8 137.9 reduce-scatter.31
where the time goes:
time: 2370 us; the launch traced here: 2340 us
  waiting for transfers between devices  1030 us (43%)
  local copies, waits for them, and re-layouts  678 us (29%)
  matrix products  408 us (17%)
  blocking collectives  91 us (4%)
  other arithmetic  72.1 us (3%)
  between operations  33.2 us (1%)
  loops' own time  27.1 us (1%)
    unnamed x27, waiting for transfers between devices  497 us
    unnamed x311, local copies, waits for them, and re-layouts  489 us
    psum x1, waiting for transfers between devices, body(): ffn_out, low_down = lax.psum((down_part, low_down_part), 'tp')  153 us
    psum x2, waiting for transfers between devices, attn_forward(): attended, low_out = lax.psum((out_part, low_part), 'tp')  141 us
    reduce_scatter x1, waiting for transfers between devices, body(): lax.psum_scatter(spread(onehot, pieces[6]), ('fsdp', 'ctx', 'tp'), scatte...  132 us
    dot_general x36, matrix products, head_scores(): jnp.einsum('sqd,skd->sqk', queries, key_part, preferred_element_type=jnp....  103 us
    all_gather x1, waiting for transfers between devices, ffn_forward(): lax.all_gather(w_gate_up, 'fsdp', axis=0, tiled=True)  51.7 us
    dot_general x24, matrix products, head_forward(): jnp.einsum('sqk,skd->sqd', weights.astype(jnp.bfloat16), value_part, pref...  51 us
  transfers between devices with their start and end apart: 20, of which 11 were waited for; matrix products, arithmetic and copies ran while one was open for 36% of the time, Pallas kernels for 0%

commit v1 on v0

v1 whole, which is shorter than its diff:
```python
import jax
import jax.numpy as jnp
from jax import lax
from jax.sharding import PartitionSpec as P

HD = 64
DOC_MOST = 800
DOCS = 8
BF = jnp.bfloat16
F32 = jnp.float32
HI = lax.Precision.HIGHEST


def dot(a, b):
    return jnp.dot(a, b, preferred_element_type=F32)


def dot_t(a, b):
    return lax.dot_general(a, b, (((1,), (1,)), ((), ())), preferred_element_type=F32)


def t_dot(a, b):
    return lax.dot_general(a, b, (((0,), (0,)), ((), ())), preferred_element_type=F32)


def xor_order(size):
    order, bit = [0], size // 2
    while bit:
        order, bit = order + [step ^ bit for step in order], bit // 2
    return order


def gather_blocks(shard, axis_name, dim):
    size = lax.axis_size(axis_name)
    pieces, bit = [shard], size // 2
    while bit:
        pairs = [(i, i ^ bit) for i in range(size)]
        pieces = pieces + [lax.ppermute(part, axis_name, pairs) for part in pieces]
        bit //= 2
    return jnp.concatenate(pieces, axis=dim)


def to_xor(values, dim, size, rank):
    block = values.shape[dim] // size
    return jnp.concatenate(
        [lax.dynamic_slice_in_dim(values, (rank ^ step) * block, block, dim) for step in xor_order(size)],
        axis=dim,
    )


def from_xor(values, dim, size, rank):
    block = values.shape[dim] // size
    bits = size.bit_length() - 1
    pieces = []
    for natural in range(size):
        mixed = rank ^ natural
        place = sum(((mixed >> j) & 1) << (bits - 1 - j) for j in range(bits))
        pieces.append(lax.dynamic_slice_in_dim(values, place * block, block, dim))
    return jnp.concatenate(pieces, axis=dim)


def rms_factor(values):
    return lax.rsqrt(jnp.mean(values * values, axis=-1, keepdims=True) + 1e-05)


def rms_back(values, gain_vec, incoming):
    factor = rms_factor(values)
    scaled = incoming * gain_vec
    return factor * scaled - values * factor**3 * jnp.mean(values * scaled, axis=-1, keepdims=True)


def heads(values):
    return values.reshape(values.shape[0], -1, HD)


def shift(values, hop, size):
    pairs = [(i, i + hop) for i in range(size) if 0 <= i + hop < size]
    return lax.ppermute(values, "ctx", pairs)


def body(
    tokens, segments, adapter_index, w_qkv, w_forget, forget_bias, w_out, w_gate_up, w_down,
    gain_attn, gain_ffn, a_qkv, b_qkv, a_out, b_out, a_gate_up, b_gate_up, a_down, b_down, cotangent,
):
    count, rows, width = tokens.shape
    assert count == 1
    head_cols = w_qkv.shape[2]
    local_heads = w_forget.shape[1]
    unit_cols = w_gate_up.shape[2]
    rank_r = a_qkv.shape[2]
    n_f, n_c, n_t = (lax.axis_size("fsdp"), lax.axis_size("ctx"), lax.axis_size("tp"))
    assert n_t == 2
    f_rank, c_rank, t_rank = (lax.axis_index("fsdp"), lax.axis_index("ctx"), lax.axis_index("tp"))
    hops = -(-(DOC_MOST - 1) // rows)
    assert hops == 2 and n_c > 1
    tail = -(-(DOC_MOST - 1 - rows) // 32) * 32
    before = hops * rows
    half = rows // 2
    swap_t = [(0, 1), (1, 0)]

    def other(values):
        return lax.ppermute(values, "tp", swap_t)

    tok_raw = tokens[0]
    prev_one = shift(tok_raw, 1, n_c)
    prev_two = shift(prev_one[rows - tail :], 1, n_c)
    tok_prev = jnp.concatenate([jnp.zeros((rows - tail, width), BF), prev_two, prev_one], axis=0)

    pick = adapter_index[0]
    take = lambda table: lax.dynamic_index_in_dim(table, pick, 0, keepdims=False)
    mix = lambda values, dim: to_xor(values, dim, n_f, f_rank)
    qkv_a, ffn_a = (mix(take(a_qkv), 0), mix(take(a_gate_up), 0))
    out_b, down_b = (mix(take(b_out), 1), mix(take(b_down), 1))
    qkv_b = lax.dynamic_slice_in_dim(take(b_qkv), t_rank * head_cols, head_cols, 2).reshape(rank_r, 3 * head_cols)
    out_a = take(a_out)
    ffn_b = lax.dynamic_slice_in_dim(take(b_gate_up), t_rank * unit_cols, unit_cols, 2).reshape(rank_r, 2 * unit_cols)
    down_a = lax.dynamic_slice_in_dim(take(a_down), t_rank * unit_cols, unit_cols, 0)
    gain_one = mix(gain_attn.astype(F32), 0)
    gain_two = mix(gain_ffn.astype(F32), 0)
    bias = forget_bias.astype(F32)

    qkv_w = gather_blocks(w_qkv.reshape(-1, 3 * head_cols), "fsdp", 0)
    forget_w = gather_blocks(w_forget, "fsdp", 0)
    out_w_own = gather_blocks(w_out, "fsdp", 1)
    out_w_other = other(out_w_own)
    first = t_rank == 0
    out_w = jnp.concatenate(
        [jnp.where(first, out_w_own, out_w_other), jnp.where(first, out_w_other, out_w_own)], axis=0
    )
    gate_up_w = gather_blocks(w_gate_up.reshape(-1, 2 * unit_cols), "fsdp", 0)
    down_w = gather_blocks(w_down, "fsdp", 1)

    seg_all = lax.all_gather(segments[0], "ctx", tiled=True)
    full = seg_all.shape[0]
    starts_of = jnp.sum(seg_all[None, :] < jnp.arange(DOCS)[:, None], axis=1)
    starts = jnp.sum(jnp.where(seg_all[:, None] == jnp.arange(DOCS)[None, :], starts_of[None, :], 0), axis=1)
    starts = jnp.concatenate([starts, jnp.full((before,), 2 * full, starts.dtype)])
    base = c_rank * rows
    start_own = lax.dynamic_slice_in_dim(starts, base, rows)
    start_next = lax.dynamic_slice_in_dim(starts, base + rows, before)
    pos_own = base + jnp.arange(rows)
    pos_keys = base - before + jnp.arange(before + rows)
    pos_next = base + rows + jnp.arange(before)
    allowed = (pos_keys[None, :] >= start_own[:, None]) & (pos_keys[None, :] <= pos_own[:, None])
    allowed_next = pos_own[None, :] >= start_next[:, None]

    def project(tok, cols_from):
        values = tok.astype(F32)
        normed = (values * rms_factor(values) * gain_one).astype(BF)
        low = dot(normed, qkv_a).astype(BF)
        proj = (dot(normed, qkv_w[:, cols_from:]) + dot(low, qkv_b[:, cols_from:])).astype(BF)
        logits = dot(normed, forget_w) + bias
        return normed, low, proj, logits

    tok_own = mix(tok_raw, 1)
    normed, low_qkv, proj, logits = project(tok_own, 0)
    _, _, proj_prev, logits_prev = project(mix(tok_prev, 1), head_cols)
    query = (proj[:, :head_cols].astype(F32) * HD ** (-0.5)).astype(BF)
    keys = jnp.concatenate([proj_prev[:, :head_cols], proj[:, head_cols : 2 * head_cols]], axis=0)
    vals = jnp.concatenate([proj_prev[:, head_cols:], proj[:, 2 * head_cols :]], axis=0)
    forget = jax.nn.log_sigmoid(logits)
    forget_prev = jax.nn.log_sigmoid(logits_prev)
    same_own = allowed[:, before:].astype(F32)
    after_own = (jnp.arange(rows)[None, :] > jnp.arange(rows)[:, None]).astype(F32)
    after_prev = (jnp.arange(before)[None, :] > jnp.arange(before)[:, None]).astype(F32)
    exact = lambda a, b: jnp.dot(a, b, precision=HI, preferred_element_type=F32)
    gates = exact(same_own, forget)
    key_gates = jnp.concatenate([-exact(after_prev, forget_prev), gates], axis=0)
    total_one = jnp.sum(forget_prev[before - rows :], axis=0)
    key_gates_next = -exact(after_own, forget)

    q_h, k_h, v_h = (heads(query), heads(keys), heads(vals))

    def score(q, k, gq, gk, ok):
        s = jnp.einsum("qhd,khd->hqk", q, k, preferred_element_type=F32)
        return jnp.where(ok[None], s + gq.T[:, :, None] - gk.T[:, None, :], -1e30)

    s = score(q_h, k_h, gates, key_gates, allowed)
    top = jnp.max(s, axis=-1, keepdims=True)
    w = jnp.exp(s - top)
    total = jnp.sum(w, axis=-1, keepdims=True)
    w = w / total
    mixed_f = jnp.einsum("hqk,khd->qhd", w.astype(BF), v_h, preferred_element_type=F32)
    log_total = (top + jnp.log(total))[:, :, 0].T
    mixed_own = mixed_f.reshape(rows, head_cols).astype(BF)
    mixed_other = other(mixed_own)
    mixed = jnp.concatenate(
        [jnp.where(first, mixed_own, mixed_other), jnp.where(first, mixed_other, mixed_own)], axis=1
    )
    q_gate = gates - log_total
    q_gate_two = (q_gate + total_one[None, :])[:tail]
    send_q1 = shift(query, -1, n_c)
    send_q2 = shift(query[:tail], -2, n_c)
    send_g1 = shift(q_gate, -1, n_c)
    send_g2 = shift(q_gate_two, -2, n_c)

    low_out = dot(mixed, out_a).astype(BF)
    hidden = tok_own.astype(F32) + dot(mixed, out_w) + dot(low_out, out_b)
    normed_ffn = (hidden * rms_factor(hidden) * gain_two).astype(BF)
    low_ffn = dot(normed_ffn, ffn_a).astype(BF)
    both = dot(normed_ffn, gate_up_w) + dot(low_ffn, ffn_b)
    gate_val, up_val = both[:, :unit_cols], both[:, unit_cols:]
    sig = jax.nn.sigmoid(gate_val)
    units = (gate_val * sig * up_val).astype(BF)
    cot = mix(cotangent[0], 1)
    grad_low_down = dot_t(cot, down_b).astype(BF)
    grad_units = dot_t(cot, down_w) + dot_t(grad_low_down, down_a)
    grad_gate = (grad_units * up_val * sig * (1.0 + gate_val * (1.0 - sig))).astype(BF)
    grad_up = (grad_units * gate_val * sig).astype(BF)
    grad_both = jnp.concatenate([grad_gate, grad_up], axis=1)
    part = dot_t(grad_both, gate_up_w)
    part_low = dot_t(grad_both, ffn_b)
    mine = t_rank * half
    theirs = (1 - t_rank) * half
    own_rows = lambda values: lax.dynamic_slice_in_dim(values, mine, half, 0)
    far_rows = lambda values: lax.dynamic_slice_in_dim(values, theirs, half, 0)
    got = other(far_rows(part).astype(BF))
    got_low = other(far_rows(part_low))
    grad_low_ffn = (own_rows(part_low) + got_low).astype(BF)
    grad_normed_ffn = own_rows(part) + got.astype(F32) + dot_t(grad_low_ffn, ffn_a)
    hidden_half = own_rows(hidden)
    grad_hidden = own_rows(cot).astype(F32) + rms_back(hidden_half, gain_two, grad_normed_ffn)
    grad_hidden_b = grad_hidden.astype(BF)
    grad_low_out = dot_t(grad_hidden_b, out_b).astype(BF)
    grad_mixed_half = (dot_t(grad_hidden_b, out_w) + dot_t(grad_low_out, out_a)).astype(BF)
    gm_own = lax.dynamic_slice_in_dim(grad_mixed_half, t_rank * head_cols, head_cols, 1)
    gm_far = other(lax.dynamic_slice_in_dim(grad_mixed_half, (1 - t_rank) * head_cols, head_cols, 1))
    grad_mixed = jnp.concatenate([jnp.where(first, gm_own, gm_far), jnp.where(first, gm_far, gm_own)], axis=0)

    d_h = heads(grad_mixed)
    delta = jnp.sum(d_h.astype(F32) * mixed_f, axis=-1)
    send_d1 = shift(grad_mixed, -1, n_c)
    send_d2 = shift(grad_mixed[:tail], -2, n_c)
    send_e1 = shift(delta, -1, n_c)
    send_e2 = shift(delta[:tail], -2, n_c)
    pad = lambda values: jnp.pad(values, ((0, rows - tail), (0, 0)))
    q_next = jnp.concatenate([send_q1, pad(send_q2)], axis=0)
    g_next = jnp.concatenate([send_g1, pad(send_g2)], axis=0)
    d_next = jnp.concatenate([send_d1, pad(send_d2)], axis=0)
    e_next = jnp.concatenate([send_e1, pad(send_e2)], axis=0)

    def back(q, k, v, d, gq, gk, e, ok):
        p = jnp.exp(score(q, k, gq, gk, ok))
        dp = jnp.einsum("qhd,khd->hqk", d, v, preferred_element_type=F32)
        return p.astype(BF), (p * (dp - e.T[:, :, None])).astype(BF)

    p_own, ds_own = back(q_h, k_h, v_h, d_h, q_gate, key_gates, delta, allowed)
    qn_h, dn_h = (heads(q_next), heads(d_next))
    p_nxt, ds_nxt = back(qn_h, k_h[before:], v_h[before:], dn_h, g_next, key_gates_next, e_next, allowed_next)
    grad_q = jnp.einsum("hqk,khd->qhd", ds_own, k_h, preferred_element_type=F32) * HD ** (-0.5)
    grad_k = jnp.einsum("hqk,qhd->khd", ds_own[:, :, before:], q_h, preferred_element_type=F32)
    grad_k = grad_k + jnp.einsum("hqk,qhd->khd", ds_nxt, qn_h, preferred_element_type=F32)
    grad_v = jnp.einsum("hqk,qhd->khd", p_own[:, :, before:], d_h, preferred_element_type=F32)
    grad_v = grad_v + jnp.einsum("hqk,qhd->khd", p_nxt, dn_h, preferred_element_type=F32)
    row_sum = jnp.sum(ds_own.astype(F32), axis=2).T
    col_own = jnp.sum(ds_own[:, :, before:].astype(F32), axis=1).T
    col_next = jnp.sum(ds_nxt.astype(F32), axis=1).T
    across = jnp.sum(ds_own[:, :, : before - rows].astype(F32), axis=(1, 2))[None, :]
    across = shift(across, -1, n_c)
    grad_forget = (
        lax.dot_general(same_own, row_sum - col_own, (((0,), (0,)), ((), ())), precision=HI, preferred_element_type=F32)
        + lax.dot_general(after_own, col_next, (((0,), (0,)), ((), ())), precision=HI, preferred_element_type=F32)
        + across
    )
    grad_logits = (grad_forget * jax.nn.sigmoid(-logits)).astype(BF)
    grad_proj = jnp.concatenate(
        [grad_q.reshape(rows, head_cols), grad_k.reshape(rows, head_cols), grad_v.reshape(rows, head_cols)], axis=1
    ).astype(BF)

    part_low_qkv = dot_t(grad_proj, qkv_b)
    grad_low_qkv = (part_low_qkv + other(part_low_qkv)).astype(BF)
    part_in = dot_t(grad_proj, qkv_w) + dot_t(grad_logits, forget_w)
    got_in = other(far_rows(part_in).astype(BF))
    grad_normed = own_rows(part_in) + got_in.astype(F32) + dot_t(own_rows(grad_low_qkv), qkv_a)
    grad_tok = (grad_hidden + rms_back(own_rows(tok_own).astype(F32), gain_one, grad_normed)).astype(BF)
    tok_far = other(grad_tok)
    grad_tok = jnp.concatenate([jnp.where(first, grad_tok, tok_far), jnp.where(first, tok_far, grad_tok)], axis=0)
    grad_tokens = from_xor(grad_tok, 1, n_f, f_rank).astype(F32)

    part_low_down = dot(units, down_a)
    low_down = (part_low_down + other(part_low_down)).astype(BF)
    part_down = dot(units, down_w).astype(BF)
    ffn_out = part_down.astype(F32) + other(part_down).astype(F32)
    block_output = from_xor((hidden + ffn_out + dot(low_down, down_b)).astype(BF), 1, n_f, f_rank)

    own_part = lambda values, n: values * (lax.broadcasted_iota(jnp.int32, (1, n), 1) // (n // 2) == t_rank)
    natural = lambda values: from_xor(values, 1, n_f, f_rank)
    place = lambda values: jnp.concatenate([jnp.where(first, values, 0.0), jnp.where(first, 0.0, values)], axis=1)
    g_b_qkv = t_dot(low_qkv, grad_proj)
    g_b_ffn = t_dot(low_ffn, grad_both)
    tables = [
        own_part(natural(t_dot(grad_low_qkv, normed)), width),
        *[place(g_b_qkv[:, i * head_cols : (i + 1) * head_cols]) for i in range(3)],
        t_dot(grad_low_out, own_rows(mixed)),
        natural(t_dot(own_rows(low_out), grad_hidden_b)),
        natural(t_dot(grad_low_ffn, own_rows(normed_ffn))),
        *[place(g_b_ffn[:, i * unit_cols : (i + 1) * unit_cols]) for i in range(2)],
        place(t_dot(grad_low_down, units)),
        own_part(natural(t_dot(low_down, cot)), width),
    ]
    packed = jnp.concatenate([t.reshape(rank_r, n_f, n_c, n_t, -1) for t in tables], axis=4)
    block = packed.shape[4]
    packed = packed.transpose(2, 1, 3, 0, 4)
    by_ctx = jnp.sum(lax.all_to_all(packed, "ctx", 0, 0, tiled=True).reshape(n_c, n_f * n_t, rank_r, block), axis=0)
    landed = lax.all_to_all(by_ctx, ("fsdp", "tp"), 0, 0, tiled=True)
    by_seq = jnp.sum(landed.reshape(n_f, n_t, rank_r, block), axis=1)
    every = lax.all_gather(adapter_index, "fsdp", tiled=True)
    onehot = (jnp.arange(a_qkv.shape[0])[:, None] == every[None, :]).astype(F32)
    spread = jnp.einsum("as,srk->ark", onehot, by_seq, precision=HI, preferred_element_type=F32)
    sizes = [t.shape[1] // (n_f * n_c * n_t) for t in tables]
    outs, at = [], 0
    for size in sizes:
        outs.append(spread[:, :, at : at + size])
        at += size
    swap = lambda values: values.transpose(0, 2, 1)
    return (
        block_output[None],
        grad_tokens[None],
        swap(outs[0]),
        jnp.stack(outs[1:4], axis=2),
        swap(outs[4]),
        outs[5],
        swap(outs[6]),
        jnp.stack(outs[7:9], axis=2),
        swap(outs[9]),
        outs[10],
    )


def solution(mesh):
    in_specs = (
        P("fsdp", "ctx", None), P("fsdp", "ctx"), P("fsdp"), P("fsdp", None, "tp"), P("fsdp", "tp"), P("tp"),
        P("tp", "fsdp"), P("fsdp", None, "tp"), P("tp", "fsdp"),
        P(), P(), P(), P(), P(), P(), P(), P(), P(), P(),
        P("fsdp", "ctx", None),
    )
    out_specs = (
        P("fsdp", "ctx", None),
        P("fsdp", "ctx", None),
        P(None, ("fsdp", "ctx", "tp"), None),
        P(None, None, None, ("fsdp", "ctx", "tp")),
        P(None, ("fsdp", "ctx", "tp"), None),
        P(None, None, ("fsdp", "ctx", "tp")),
        P(None, ("fsdp", "ctx", "tp"), None),
        P(None, None, None, ("fsdp", "ctx", "tp")),
        P(None, ("fsdp", "ctx", "tp"), None),
        P(None, None, ("fsdp", "ctx", "tp")),
    )
    return jax.shard_map(body, mesh=mesh, in_specs=in_specs, out_specs=out_specs, check_vma=False)
```

time: 2370 us -> 728 us (0.31)
  waiting for transfers between devices: 1030 us -> 181 us
  local copies, waits for them, and re-layouts: 678 us -> 119 us
  matrix products: 408 us -> 233 us
  blocking collectives: 91 us -> 33.1 us
  starting transfers between devices: 1.43 us -> 47.8 us
  between operations: 33.2 us -> 3.53 us
  other arithmetic: 72.1 us -> 100 us
  loops' own time: 27.1 us -> 0 us
    unnamed x27 -> x0, waiting for transfers between devices: 497 us -> none
    unnamed x311 -> x267, local copies, waits for them, and re-layouts: 489 us -> 47.1 us
    psum x3 -> x0, waiting for transfers between devices: 294 us -> none  [the longest x1 153 us: body(): ffn_out, low_down = lax.psum((down_part, low_down_part), 'tp')]
    dot_general x155 -> x53, matrix products: 408 us -> 233 us  [the longest x16 56.4 us: dot(): return jnp.dot(a, b, preferred_element_type=F32)]
    ppermute x0 -> x36, waiting for transfers between devices: none -> 162 us  [the longest x10 72.8 us: other(): return lax.ppermute(values, 'tp', swap_t)]
    reduce_scatter x4 -> x0, waiting for transfers between devices: 132 us -> none  [the longest x1 132 us: body(): lax.psum_scatter(spread(onehot, pieces[6]), ('fsdp', 'ctx', 'tp'), scatte...]
    all_gather x6 -> x0, waiting for transfers between devices: 107 us -> none  [the longest x1 51.7 us: ffn_forward(): lax.all_gather(w_gate_up, 'fsdp', axis=0, tiled=True)]
    dynamic_update_slice x37 -> x0, local copies, waits for them, and re-layouts: 41.2 us -> none  [the longest x24 23 us: attn_forward(): lax.map(lambda head_item: head_forward(head_item, allowed), (to_heads(pro...]
  transfers between devices with their start and end apart: 20 -> 38, of which waited for: 11 -> 11; matrix products, arithmetic and copies ran while one was open for 36% -> 55% of each run, Pallas kernels for 0% -> 0%
where the time goes in v1:
time: 728 us; the launch traced here: 718 us
  matrix products  233 us (32%)
  waiting for transfers between devices  181 us (25%)
  local copies, waits for them, and re-layouts  119 us (16%)
  other arithmetic  100 us (14%)
  starting transfers between devices  47.8 us (7%)
  blocking collectives  33.1 us (5%)
    ppermute x10, waiting for transfers between devices, other(): return lax.ppermute(values, 'tp', swap_t)  72.8 us
    ppermute x15, waiting for transfers between devices, gather_blocks(): pieces = pieces + [lax.ppermute(part, axis_name, pairs) for part in pieces]  72 us
    dot_general x16, matrix products, dot(): return jnp.dot(a, b, preferred_element_type=F32)  56.4 us
    dot_general x13, matrix products, dot_t(): lax.dot_general(a, b, (((1,), (1,)), ((), ())), preferred_element_type=F32)  47.3 us
    unnamed x267, local copies, waits for them, and re-layouts  47.1 us
    dot_general x2, matrix products, back(): dp = jnp.einsum('qhd,khd->hqk', d, v, preferred_element_type=F32)  36.4 us
    exp x1, other arithmetic, back(): p = jnp.exp(score(q, k, gq, gk, ok))  29.1 us
    all_gather x1, blocking collectives, body(): seg_all = lax.all_gather(segments[0], 'ctx', tiled=True)  28.3 us
  transfers between devices with their start and end apart: 38, of which 11 were waited for; matrix products, arithmetic and copies ran while one was open for 55% of the time, Pallas kernels for 0%

profile of v1, /device:TPU:0, one launch (start us, length us, event | category | flops | bytes accessed | tf_op | source)
XLA Modules:
  0.0 717.6 jit_solution(6308257292521335504)
XLA Ops:
  21.6 28.3 %all-gather = s32[1,2048]{1,0:T(1,128)S(1)} all-gather(s32[1,512]{1,0:T(1,128)S(1)} %copy-done.108), channel_id=2, replica_groups=mesh['fsdp'=4,'ctx'=4,'tp'=2] {'ctx'}, dimensions={1}, use_global_device_ids=true | all-gather | bytes 10240 | tf_op jit(solution)/shard_map/all_gather | solution.py:133
  111.4 22.6 %collective-permute-done.2 = bf16[384,2304]{0,1:T(8,128)(2,1)} collective-permute-done((bf16[384,2304]{0,1:T(8,128)(2,1)}, bf16[384,2304]{0,1:T(8,128)(2,1)}, u32[]{:S(2)}, u32[]{:S(2)}) %collective-permute-start.2) | collective-permute-done | bytes 1769504 | tf_op jit(solution)/shard_map/ppermute | solution.py:38
  151.4 49.2 %collective-permute-done.13 = bf16[384,4096]{1,0:T(8,128)(2,1)} collective-permute-done((bf16[384,4096]{1,0:T(8,128)(2,1)}, bf16[384,4096]{1,0:T(8,128)(2,1)}, u32[]{:S(2)}, u32[]{:S(2)}) %collective-permute-start.13) | collective-permute-done | bytes 3145760 | tf_op jit(solution)/shard_map/ppermute | solution.py:38
  220.9 10.2 %add_convert_fusion = bf16[1024,1536]{1,0:T(8,128)(2,1)S(1)} fusion(f32[1024,1536]{1,0:T(8,128)} %fusion.50, bf16[384,2304]{0,1:T(8,128)(2,1)} %collective-permute-done.4, bf16[384,2304]{0,1:T(8,128)(2,1)} %collective-permute-done.3, bf16[384,2304]{0,1:T(8,128)(2,1)} %collective-permute-done.2, bf16[384,2304]{0,1:T(8,128)(2,1)} %bitcast.5, ...), kind=kOutput, calls=%fused_computation.25 | convolution fusion | flops 4871159808 | bytes 19671040 | tf_op jit(solution)/shard_map/dot_general | solution.py:15
  238.4 17.9 %fusion.1 = (f32[12,512]{1,0:T(8,128)S(1)}, f32[12,512,1536]{2,1,0:T(8,128)}) fusion(f32[12,1536]{1,0:T(8,128)S(1)} %maximum_bitcast_fusion.1, f32[12,512]{1,0:T(8,128)S(1)} %bitcast.229, pred[512,1536]{1,0:T(8,128)(4,1)S(1)} %compare_and_fusion, bf16[512,12,64]{0,2,1:T(8,128)(2,1)} %bitcast.214, bf16[1536,12,64]{0,2,1:T(8,128)(2,1)} %bitcast.204), kind=kOutput, calls=%fused_computation.10 | convolution fusion | flops 1245702144 | bytes 41803776 | tf_op jit(solution)/shard_map/qhd,khd->hqk/dot_general | solution.py:175
  256.4 18.7 %fusion = f32[12,512]{1,0:T(8,128)S(1)} fusion(f32[12,512,1536]{2,1,0:T(8,128)} %get-tuple-element.193, f32[12,512]{1,0:T(8,128)S(1)} %get-tuple-element.192, f32[12,1536]{1,0:T(8,128)S(1)} %maximum_bitcast_fusion.1, f32[12,512]{1,0:T(8,128)S(1)} %bitcast.230, pred[512,1536]{1,0:T(8,128)(4,1)S(1)} %compare_and_fusion), kind=kLoop, calls=%fused_computation.6 | loop fusion | flops 47179776 | bytes 38682624 | tf_op jit(solution)/shard_map/reduce_sum | solution.py:181
  281.0 18.2 %bitcast_convert_fusion = (bf16[512,12,64]{0,2,1:T(8,128)(2,1)}, f32[12,64,512]{2,1,0:T(8,128)}) fusion(bf16[1536,12,64]{0,2,1:T(8,128)(2,1)} %bitcast.209, f32[12,512,1536]{2,1,0:T(8,128)} %get-tuple-element.193, f32[12,512]{1,0:T(8,128)S(1)} %fusion, f32[12,512]{1,0:T(8,128)S(1)} %get-tuple-element.192, f32[12,1536]{1,0:T(8,128)S(1)} %maximum_bitcast_fusion.1, ...), kind=kOutput, calls=%fused_computation.101 | convolution fusion | flops 1264975872 | bytes 43401216 | tf_op jit(solution)/shard_map/hqk,khd->qhd/dot_general | solution.py:183
  303.3 29.1 %select_exponential_fusion = f32[12,512,1536]{2,1,0:T(8,128)} fusion(f32[12,512,1536]{2,1,0:T(8,128)} %get-tuple-element.193, f32[12,512]{1,0:T(8,128)S(1)} %fusion.101, f32[12,1536]{1,0:T(8,128)S(1)} %maximum_bitcast_fusion.1, pred[512,1536]{1,0:T(8,128)(4,1)S(1)} %compare_and_fusion), kind=kLoop, calls=%fused_computation.2 | loop fusion | flops 28311552 | bytes 76382208 | tf_op jit(solution)/shard_map/exp | solution.py:243
  356.9 10.2 %fusion.163 = f32[12,1024,512]{2,1,0:T(8,128)} fusion(bf16[1024,12,64]{0,2,1:T(8,128)(2,1)S(1)} %bitcast.202, bf16[512,12,64]{0,2,1:T(8,128)(2,1)S(1)} %bitcast.211), kind=kOutput, calls=%fused_computation.389 | convolution fusion | flops 805306368 | bytes 27525120 | tf_op jit(solution)/shard_map/qhd,khd->hqk/dot_general | solution.py:175
  371.3 12.1 %convolution_add_fusion = f32[512,4096]{1,0:T(8,128)} fusion(f32[512,4096]{1,0:T(8,128)S(1)} %fusion.162, bf16[512,1536]{1,0:T(8,128)(2,1)S(1)} %multiply_convert_fusion.5, bf16[1536,4096]{1,0:T(8,128)(2,1)} %constant_dynamic-update-slice_fusion.8), kind=kOutput, calls=%fused_computation.26 | convolution fusion | flops 6444548096 | bytes 30932992 | tf_op jit(solution)/shard_map/dot_general | solution.py:15
  383.4 8.8 %multiply_convert_fusion.3 = (bf16[512,2048]{1,0:T(8,128)(2,1)}, bf16[512,2048]{1,0:T(8,128)(2,1)}, bf16[512,2048]{1,0:T(8,128)(2,1)S(1)}) fusion(f32[512,4096]{1,0:T(8,128)} %convolution_add_fusion, f32[512,2048]{1,0:T(8,128)S(1)} %copy-done.27, bf16[512,1536]{1,0:T(8,128)(2,1)S(1)} %copy-done.13, bf16[2048,1536]{1,0:T(8,128)(2,1)S(1)} %bitcast.234), kind=kOutput, calls=%fused_computation.45 | convolution fusion | flops 3239051264 | bytes 26738688 | tf_op jit(solution)/shard_map/dot_general | solution.py:19
  398.5 11.3 %fusion.47 = f32[512,1536]{1,0:T(8,128)S(1)} fusion(bf16[1536,4096]{1,0:T(8,128)(2,1)} %constant_dynamic-update-slice_fusion.8, bf16[512,2048]{1,0:T(8,128)(2,1)} %get-tuple-element.89, bf16[512,2048]{1,0:T(8,128)(2,1)S(1)} %copy-done.113), kind=kOutput, calls=%fused_computation.116 | convolution fusion | flops 6450839552 | bytes 19922944 | tf_op jit(solution)/shard_map/dot_general | solution.py:19
  418.5 48.7 %collective-permute-done.22 = f32[256,16]{0,1:T(8,128)} collective-permute-done((f32[256,16]{0,1:T(8,128)S(1)}, f32[256,16]{0,1:T(8,128)}, u32[]{:S(2)}, u32[]{:S(2)}) %collective-permute-start.22) | collective-permute-done | bytes 16416 | tf_op jit(solution)/shard_map/ppermute | solution.py:102
  491.7 6.9 collective-permute-done.23
  505.3 6.9 fusion.10
  512.2 21.5 %convert_reduce_fusion = (f32[12,512]{1,0:T(8,128)S(1)}, bf16[12,512,1536]{2,1,0:T(8,128)(2,1)}) fusion(f32[12,512,1536]{2,1,0:T(8,128)} %select_exponential_fusion, f32[12,512]{1,0:T(8,128)S(1)} %bitcast.239, bf16[512,12,64]{0,2,1:T(8,128)(2,1)S(1)} %bitcast.208, bf16[1536,12,64]{0,2,1:T(8,128)(2,1)S(1)} %bitcast.210), kind=kOutput, calls=%fused_computation | convolution fusion | flops 1255139328 | bytes 59817984 | tf_op jit(solution)/shard_map/qhd,khd->hqk/dot_general | solution.py:244
  540.1 9.8 %multiply_convert_fusion.6 = bf16[12,64,512]{2,1,0:T(8,128)(2,1)S(1)} fusion(bf16[1536,12,64]{0,2,1:T(8,128)(2,1)S(1)} %bitcast.205, bf16[12,512,1536]{2,1,0:T(8,128)(2,1)} %get-tuple-element.200), kind=kOutput, calls=%fused_computation.107 | convolution fusion | flops 1208745984 | bytes 22020096 | tf_op jit(solution)/shard_map/hqk,khd->qhd/dot_general | solution.py:250
  559.6 17.1 %collective-permute-done.31 = f32[288,12]{0,1:T(8,128)S(1)} collective-permute-done((f32[288,12]{0,1:T(8,128)S(1)}, f32[288,12]{0,1:T(8,128)S(1)}, u32[]{:S(2)}, u32[]{:S(2)}) %collective-permute-start.31) | collective-permute-done | bytes 13856 | tf_op jit(solution)/shard_map/ppermute | solution.py:78
  580.2 12.7 %add_convert_fusion.2 = bf16[12,64,512]{2,1,0:T(8,128)(2,1)S(1)} fusion(f32[12,64,512]{2,1,0:T(8,128)} %fusion.10, bf16[1024,12,64]{0,2,1:T(8,128)(2,1)} %bitcast.220, f32[12,1024,512]{2,1,0:T(8,128)} %fusion.163, f32[12,512]{1,0:T(8,128)} %convolution_negate_fusion, f32[12,1024]{1,0:T(8,128)S(1)} %copy-done.96, pred[1024,512]{1,0:T(8,128)(4,1)} %broadcast_compare_fusion), kind=kOutput, calls=%fused_computation.105 | convolution fusion | flops 831258624 | bytes 29696000 | tf_op jit(solution)/shard_map/hqk,qhd->khd/dot_general | solution.py:254
  593.0 14.9 %convert_reduce_fusion.1 = (f32[12,512]{1,0:T(8,128)S(1)}, bf16[12,1024,512]{2,1,0:T(8,128)(2,1)S(1)}) fusion(f32[12,1024]{1,0:T(8,128)S(1)} %fusion.72, bf16[1024,12,64]{0,2,1:T(8,128)(2,1)S(1)} %bitcast.221, bf16[512,12,64]{0,2,1:T(8,128)(2,1)S(1)} %bitcast.226, f32[12,512]{1,0:T(8,128)S(1)} %copy-done.115, f32[12,1024,512]{2,1,0:T(8,128)} %fusion.163, ...), kind=kOutput, calls=%fused_computation.7 | convolution fusion | flops 855631872 | bytes 40779776 | tf_op jit(solution)/shard_map/qhd,khd->hqk/dot_general | solution.py:244
  613.1 11.5 %convolution_add_fusion.2 = f32[512,1536]{1,0:T(8,128)S(1)} fusion(f32[512,1536]{1,0:T(8,128)S(1)} %fusion.96, bf16[384,2304]{0,1:T(8,128)(2,1)} %collective-permute-done.4, bf16[384,2304]{0,1:T(8,128)(2,1)} %collective-permute-done.3, bf16[384,2304]{0,1:T(8,128)(2,1)} %collective-permute-done.2, bf16[384,2304]{0,1:T(8,128)(2,1)} %bitcast.5, ...), kind=kOutput, calls=%fused_computation.50 | convolution fusion | flops 3660054528 | bytes 15728640 | tf_op jit(solution)/shard_map/dot_general | solution.py:19
  649.7 8.0 %concatenate.213 = f32[16,4,4,2,768]{4,3,1,0,2:T(2,128)} concatenate(f32[16,4,4,2,48]{4,3,1,0,2:T(2,128)S(1)} %copy.200, f32[16,4,4,2,48]{4,3,1,0,2:T(2,128)} %copy.201, f32[16,4,4,2,48]{4,3,1,0,2:T(2,128)} %copy.202, f32[16,4,4,2,48]{4,3,1,0,2:T(2,128)} %copy.203, f32[16,4,4,2,48]{4,3,1,0,2:T(2,128)} %copy.204, f32[16,4,4,2,48]{4,3,1,0,2:T(2,128)} %copy.205, ...), dimensions={4} | concatenate | bytes 3145728 | tf_op jit(solution)/shard_map/concatenate | solution.py:301
  672.3 11.8 %collective-permute-done.35 = bf16[256,1536]{1,0:T(8,128)(2,1)S(1)} collective-permute-done((bf16[256,1536]{1,0:T(8,128)(2,1)S(1)}, bf16[256,1536]{1,0:T(8,128)(2,1)S(1)}, u32[]{:S(2)}, u32[]{:S(2)}) %collective-permute-start.35) | collective-permute-done | bytes 786464 | tf_op jit(solution)/shard_map/ppermute | solution.py:102
  684.2 13.1 %all-to-all-done = f32[4,4,2,16,768]{4,2,1,3,0:T(2,128)} async-done(((f32[4,4,2,16,768]{4,2,1,3,0:T(2,128)}), f32[4,4,2,16,768]{4,2,1,3,0:T(2,128)}, u32[]{:S(2)}, u32[]{:S(2)}) %all-to-all-start) | async-done | bytes 1572896 | tf_op jit(solution)/shard_map/all_to_all | solution.py:304
  (517 shorter events, 294.5 us)
Async XLA Ops:
  0.7 90.1 %collective-permute-start.5 = (bf16[384,12]{0,1:T(8,128)(2,1)}, bf16[384,12]{0,1:T(8,128)(2,1)}, u32[]{:S(2)}, u32[]{:S(2)}) collective-permute-start(bf16[384,12]{0,1:T(8,128)(2,1)} %param.24), channel_id=1, source_target_pairs={{0,16},{8,24},{16,0},{24,8},{1,17},{9,25},{17,1},{25,9},{2,18},{10... | collective-permute-start | bytes 27656 | tf_op jit(solution)/shard_map/ppermute | solution.py:38
  3.7 87.9 %collective-permute-start.6 = (bf16[384,12]{0,1:T(8,128)(2,1)}, bf16[384,12]{0,1:T(8,128)(2,1)}, u32[]{:S(2)}, u32[]{:S(2)}) collective-permute-start(bf16[384,12]{0,1:T(8,128)(2,1)} %param.24), channel_id=1, source_target_pairs={{0,8},{8,0},{16,24},{24,16},{1,9},{9,1},{17,25},{25,17},{2,10},{10... | collective-permute-start | bytes 27656 | tf_op jit(solution)/shard_map/ppermute | solution.py:38
  3.7 91.1 %collective-permute-start = (bf16[512,1536]{1,0:T(8,128)(2,1)}, bf16[512,1536]{1,0:T(8,128)(2,1)}, u32[]{:S(2)}, u32[]{:S(2)}) collective-permute-start(bf16[512,1536]{1,0:T(8,128)(2,1)} %bitcast.222), channel_id=1, source_target_pairs={{0,2},{2,4},{4,6},{1,3},{3,5},{5,7},{8,10},{10,12},{12,14},{9,11},... | collective-permute-start | bytes 4718600 | tf_op jit(solution)/shard_map/ppermute | solution.py:78
  8.3 85.8 %collective-permute-start.9 = (bf16[768,384]{1,0:T(8,128)(2,1)}, bf16[768,384]{1,0:T(8,128)(2,1)}, u32[]{:S(2)}, u32[]{:S(2)}) collective-permute-start(bf16[768,384]{1,0:T(8,128)(2,1)} %param.26), channel_id=1, source_target_pairs={{0,16},{8,24},{16,0},{24,8},{1,17},{9,25},{17,1},{25,9},{2,18},{10... | collective-permute-start | bytes 1769480 | tf_op jit(solution)/shard_map/ppermute | solution.py:38
  9.0 97.0 %collective-permute-start.16 = (bf16[2048,384]{1,0:T(8,128)(2,1)}, bf16[2048,384]{1,0:T(8,128)(2,1)}, u32[]{:S(2)}, u32[]{:S(2)}) collective-permute-start(bf16[2048,384]{1,0:T(8,128)(2,1)} %param.28), channel_id=1, source_target_pairs={{0,16},{8,24},{16,0},{24,8},{1,17},{9,25},{17,1},{25,9},{2,18},{10... | collective-permute-start | bytes 4718600 | tf_op jit(solution)/shard_map/ppermute | solution.py:38
  92.2 41.8 %collective-permute-start.2 = (bf16[384,2304]{0,1:T(8,128)(2,1)}, bf16[384,2304]{0,1:T(8,128)(2,1)}, u32[]{:S(2)}, u32[]{:S(2)}) collective-permute-start(bf16[384,2304]{0,1:T(8,128)(2,1)} %bitcast.5), channel_id=1, source_target_pairs={{0,16},{8,24},{16,0},{24,8},{1,17},{9,25},{17,1},{25,9},{2,18},{10... | collective-permute-start | bytes 5308424 | tf_op jit(solution)/shard_map/ppermute | solution.py:38
  98.2 35.8 %collective-permute-start.1 = (bf16[288,1536]{1,0:T(8,128)(2,1)S(1)}, bf16[288,1536]{1,0:T(8,128)(2,1)S(1)}, u32[]{:S(2)}, u32[]{:S(2)}) collective-permute-start(bf16[288,1536]{1,0:T(8,128)(2,1)S(1)} %slice.151), channel_id=1, source_target_pairs={{0,2},{2,4},{4,6},{1,3},{3,5},{5,7},{8,10},{10,12},{12,14},{9,11},... | collective-permute-start | bytes 2654216 | tf_op jit(solution)/shard_map/ppermute | solution.py:78
  105.1 103.4 %collective-permute-start.3 = (bf16[384,2304]{0,1:T(8,128)(2,1)}, bf16[384,2304]{0,1:T(8,128)(2,1)}, u32[]{:S(2)}, u32[]{:S(2)}) collective-permute-start(bf16[384,2304]{0,1:T(8,128)(2,1)} %bitcast.5), channel_id=1, source_target_pairs={{0,8},{8,0},{16,24},{24,16},{1,9},{9,1},{17,25},{25,17},{2,10},{10... | collective-permute-start | bytes 5308424 | tf_op jit(solution)/shard_map/ppermute | solution.py:38
  106.0 94.6 %collective-permute-start.13 = (bf16[384,4096]{1,0:T(8,128)(2,1)}, bf16[384,4096]{1,0:T(8,128)(2,1)}, u32[]{:S(2)}, u32[]{:S(2)}) collective-permute-start(bf16[384,4096]{1,0:T(8,128)(2,1)} %bitcast.80), channel_id=1, source_target_pairs={{0,16},{8,24},{16,0},{24,8},{1,17},{9,25},{17,1},{25,9},{2,18},{10... | collective-permute-start | bytes 9437192 | tf_op jit(solution)/shard_map/ppermute | solution.py:38
  109.8 94.7 %collective-permute-start.14 = (bf16[384,4096]{1,0:T(8,128)(2,1)}, bf16[384,4096]{1,0:T(8,128)(2,1)}, u32[]{:S(2)}, u32[]{:S(2)}) collective-permute-start(bf16[384,4096]{1,0:T(8,128)(2,1)} %bitcast.80), channel_id=1, source_target_pairs={{0,8},{8,0},{16,24},{24,16},{1,9},{9,1},{17,25},{25,17},{2,10},{10... | collective-permute-start | bytes 9437192 | tf_op jit(solution)/shard_map/ppermute | solution.py:38
  134.0 74.5 %collective-permute-start.4 = (bf16[384,2304]{0,1:T(8,128)(2,1)}, bf16[384,2304]{0,1:T(8,128)(2,1)}, u32[]{:S(2)}, u32[]{:S(2)}) collective-permute-start(bf16[384,2304]{0,1:T(8,128)(2,1)} %collective-permute-done.2), channel_id=1, source_target_pairs={{0,8},{8,0},{16,24},{24,16},{1,9},{9,1},{17,25},{25,17},{2,10},{10... | collective-permute-start | bytes 5308424 | tf_op jit(solution)/shard_map/ppermute | solution.py:38
  147.0 185.4 %collective-permute-start.12 = (bf16[768,1536]{1,0:T(8,128)(2,1)}, bf16[768,1536]{1,0:T(8,128)(2,1)}, u32[]{:S(2)}, u32[]{:S(2)}) collective-permute-start(bf16[768,1536]{1,0:T(8,128)(2,1)} %constant_dynamic-update-slice_fusion.4), channel_id=1, source_target_pairs={{0,1},{1,0},{2,3},{3,2},{4,5},{5,4},{6,7},{7,6},{8,9},{9,8},{10,11... | collective-permute-start | bytes 7077896 | tf_op jit(solution)/shard_map/ppermute | solution.py:102
  219.6 121.7 %collective-permute-start.24 = (bf16[512,768]{1,0:T(8,128)(2,1)}, bf16[512,768]{1,0:T(8,128)(2,1)}, u32[]{:S(2)}, u32[]{:S(2)}) collective-permute-start(bf16[512,768]{1,0:T(8,128)(2,1)} %multiply_convert_fusion.7), channel_id=1, source_target_pairs={{2,0},{4,2},{6,4},{3,1},{5,3},{7,5},{10,8},{12,10},{14,12},{11,9},... | collective-permute-start | bytes 2359304 | tf_op jit(solution)/shard_map/ppermute | solution.py:78
  299.2 46.7 %collective-permute-start.8 = (bf16[512,768]{0,1:T(8,128)(2,1)}, bf16[512,768]{0,1:T(8,128)(2,1)}, u32[]{:S(2)}, u32[]{:S(2)}) collective-permute-start(bf16[512,768]{0,1:T(8,128)(2,1)} %bitcast.18), channel_id=1, source_target_pairs={{0,1},{1,0},{2,3},{3,2},{4,5},{5,4},{6,7},{7,6},{8,9},{9,8},{10,11... | collective-permute-start | bytes 2359304 | tf_op jit(solution)/shard_map/ppermute | solution.py:102
  300.7 40.6 %collective-permute-start.25 = (bf16[288,768]{1,0:T(8,128)(2,1)S(1)}, bf16[288,768]{1,0:T(8,128)(2,1)}, u32[]{:S(2)}, u32[]{:S(2)}) collective-permute-start(bf16[288,768]{1,0:T(8,128)(2,1)S(1)} %slice.162), channel_id=1, source_target_pairs={{4,0},{6,2},{5,1},{7,3},{12,8},{14,10},{13,9},{15,11},{20,16},{22,... | collective-permute-start | bytes 1327112 | tf_op jit(solution)/shard_map/ppermute | solution.py:78
  302.0 38.6 %collective-permute-start.26 = (f32[512,12]{0,1:T(8,128)S(1)}, f32[512,12]{0,1:T(8,128)S(1)}, u32[]{:S(2)}, u32[]{:S(2)}) collective-permute-start(f32[512,12]{0,1:T(8,128)S(1)} %bitcast_subtract_fusion), channel_id=1, source_target_pairs={{2,0},{4,2},{6,4},{3,1},{5,3},{7,5},{10,8},{12,10},{14,12},{11,9},... | collective-permute-start | bytes 73736 | tf_op jit(solution)/shard_map/ppermute | solution.py:78
  412.3 59.3 %collective-permute-start.20 = (f32[512,16]{0,1:T(8,128)S(1)}, f32[512,16]{0,1:T(8,128)}, u32[]{:S(2)}, u32[]{:S(2)}) collective-permute-start(f32[512,16]{0,1:T(8,128)S(1)} %fusion.76), channel_id=1, source_target_pairs={{0,1},{1,0},{2,3},{3,2},{4,5},{5,4},{6,7},{7,6},{8,9},{9,8},{10,11... | collective-permute-start | bytes 98312 | tf_op jit(solution)/shard_map/ppermute | solution.py:102
  412.8 254.5 %collective-permute-start.19 = (bf16[512,1536]{1,0:T(8,128)(2,1)}, bf16[512,1536]{1,0:T(8,128)(2,1)}, u32[]{:S(2)}, u32[]{:S(2)}) collective-permute-start(bf16[512,1536]{1,0:T(8,128)(2,1)} %convolution_convert_fusion), channel_id=1, source_target_pairs={{0,1},{1,0},{2,3},{3,2},{4,5},{5,4},{6,7},{7,6},{8,9},{9,8},{10,11... | collective-permute-start | bytes 4718600 | tf_op jit(solution)/shard_map/ppermute | solution.py:102
  415.3 63.6 %collective-permute-start.21 = (bf16[256,1536]{1,0:T(8,128)(2,1)}, bf16[256,1536]{1,0:T(8,128)(2,1)S(1)}, u32[]{:S(2)}, u32[]{:S(2)}) collective-permute-start(bf16[256,1536]{1,0:T(8,128)(2,1)} %dynamic-slice_convert_fusion.1), channel_id=1, source_target_pairs={{0,1},{1,0},{2,3},{3,2},{4,5},{5,4},{6,7},{7,6},{8,9},{9,8},{10,11... | collective-permute-start | bytes 2359304 | tf_op jit(solution)/shard_map/ppermute | solution.py:102
  415.8 51.4 %collective-permute-start.22 = (f32[256,16]{0,1:T(8,128)S(1)}, f32[256,16]{0,1:T(8,128)}, u32[]{:S(2)}, u32[]{:S(2)}) collective-permute-start(f32[256,16]{0,1:T(8,128)S(1)} %constant_dynamic-slice_fusion.19), channel_id=1, source_target_pairs={{0,1},{1,0},{2,3},{3,2},{4,5},{5,4},{6,7},{7,6},{8,9},{9,8},{10,11... | collective-permute-start | bytes 49160 | tf_op jit(solution)/shard_map/ppermute | solution.py:102
  500.8 77.2 %collective-permute-start.28 = (bf16[512,768]{1,0:T(8,128)(2,1)S(1)}, bf16[512,768]{1,0:T(8,128)(2,1)S(1)}, u32[]{:S(2)}, u32[]{:S(2)}) collective-permute-start(bf16[512,768]{1,0:T(8,128)(2,1)S(1)} %pad_maximum_fusion.24), channel_id=1, source_target_pairs={{2,0},{4,2},{6,4},{3,1},{5,3},{7,5},{10,8},{12,10},{14,12},{11,9},... | collective-permute-start | bytes 2359304 | tf_op jit(solution)/shard_map/ppermute | solution.py:78
  503.8 74.1 %collective-permute-start.30 = (f32[512,12]{0,1:T(8,128)S(1)}, f32[512,12]{0,1:T(8,128)S(1)}, u32[]{:S(2)}, u32[]{:S(2)}) collective-permute-start(f32[512,12]{0,1:T(8,128)S(1)} %fusion.42), channel_id=1, source_target_pairs={{2,0},{4,2},{6,4},{3,1},{5,3},{7,5},{10,8},{12,10},{14,12},{11,9},... | collective-permute-start | bytes 73736 | tf_op jit(solution)/shard_map/ppermute | solution.py:78
  576.7 35.8 %collective-permute-start.32 = (f32[1,12]{1,0:T(1,128)S(1)}, f32[1,12]{1,0:T(1,128)S(1)}, u32[]{:S(2)}, u32[]{:S(2)}) collective-permute-start(f32[1,12]{1,0:T(1,128)S(1)} %bitcast.242), channel_id=1, source_target_pairs={{2,0},{4,2},{6,4},{3,1},{5,3},{7,5},{10,8},{12,10},{14,12},{11,9},... | collective-permute-start | bytes 152 | tf_op jit(solution)/shard_map/ppermute | solution.py:78
  657.7 39.6 %all-to-all-start = ((f32[4,4,2,16,768]{4,2,1,3,0:T(2,128)}), f32[4,4,2,16,768]{4,2,1,3,0:T(2,128)}, u32[]{:S(2)}, u32[]{:S(2)}) async-start(f32[4,4,2,16,768]{4,2,1,3,0:T(2,128)} %bitcast.61), calls=%async_computation | async-start | bytes 3145728 | tf_op jit(solution)/shard_map/all_to_all | solution.py:304
  (134 other events, 1905.9 us)
